TPU v7x, 32 devices: a whole 2x2x4 slice. The times are simulated.
32 devices in a mesh: parts: 2 (over y), seq: 8 (over z, core), rep: 2 (over x), head: 1.
Axes of the slice: x: 2, y: 2, z: 4, core: 2. Of those that a mesh axis runs over, the one named last changes fastest.
Arguments:
- activations: bfloat16 [4, 1024, 2048], P(('parts', 'rep'), 'seq', 'head'), parts along dimension 0, may hold values from -6 to 6
- value_weight: bfloat16 [2048, 2048], P(('seq', 'rep'), 'head'), may hold values from -0.125 to 0.125
- query_in: bfloat16 [4, 1024, 2048], P(('parts', 'rep'), 'seq', 'head'), parts along dimension 0, may hold values from -6 to 6
- key_in: bfloat16 [4, 1024, 2048], P(('parts', 'rep'), 'seq', 'head'), parts along dimension 0, may hold values from -6 to 6
- grad_out: bfloat16 [4, 1024, 2048], P(('parts', 'rep'), 'seq', 'head'), parts along dimension 0, may hold values from -6 to 6
- conv_kernel: float32 [3, 4, 2048], P(None, None, 'head'), may hold values from -3 to 3
- log_gate: float32 [4, 16, 1024], P(('parts', 'rep'), 'head', 'seq'), parts along dimension 0, as said below
Outputs:
- attn_out: bfloat16 [4, 1024, 2048], P(('parts', 'rep'), 'seq', 'head'), parts along dimension 0
- grad_query: bfloat16 [4, 1024, 2048], P(('parts', 'rep'), 'seq', 'head'), parts along dimension 0
- grad_key: bfloat16 [4, 1024, 2048], P(('parts', 'rep'), 'seq', 'head'), parts along dimension 0
- grad_x: bfloat16 [4, 1024, 2048], P(('parts', 'rep'), 'seq', 'head'), parts along dimension 0
- grad_w: float32 [4096, 2048], P(('parts', 'seq', 'rep'), 'head'), parts along dimension 0
- grad_conv: float32 [6, 4, 2048], P('parts', None, 'head'), parts along dimension 0
There are 2 independent parts, one for each index of `parts`. A program takes and returns all parts, laid end to end along the dimension named above; an argument that names none is the same for every part. Nothing has to cross between parts.
Inputs may be any that keep to these rules, and one draw needn't show every extreme that they name: `log_gate`: every entry is below zero.
All inputs are finite; a program needn't handle non-finite values.
Results may differ from a plain program's by a relative error of at most 0.015.
Values may be sent and summed in bfloat16 or wider, within the bound.
A program may use at most 128 MiB of HBM per device.

v0:
```python
import math
import jax
import jax.numpy as jnp
from jax import lax
from jax.sharding import PartitionSpec as P

EPSILON = 1e-06


def shifted(block, axis, distance):
    devices = range(lax.axis_size(axis))
    route = [(i - distance, i) for i in devices if i - distance in devices]
    return lax.ppermute(block, axis, route)


def prefix(part, axis, combine, identity, reverse):
    count = lax.axis_size(axis)
    place = lax.axis_index(axis)
    ahead = count - 1 - place if reverse else place
    gathered = jax.tree.map(lambda a: lax.all_gather(a, axis), part)
    state = jax.tree.map(lambda a, e: jnp.zeros_like(a) + jnp.asarray(e, a.dtype), part, identity)

    def one(step, state):
        source = count - 1 - step if reverse else step
        return combine(
            state, jax.tree.map(lambda a: lax.dynamic_index_in_dim(a, source, 0, False), gathered)
        )

    return lax.fori_loop(0, ahead, one, state)


def carried_in(value, axis, combine, identity, reverse):
    length, mine = (lax.axis_size(axis), lax.axis_index(axis))
    everything = jax.tree.map(
        lambda part, kind: lax.all_gather(part.astype(kind), axis),
        value,
        (jnp.bfloat16, jnp.bfloat16),
    )
    start = jax.tree.map(
        lambda part, zero: jnp.broadcast_to(jnp.asarray(zero, part.dtype), part.shape),
        value,
        identity,
    )

    def step(k, before):
        at = length - 1 - k if reverse else k
        reached = at > mine if reverse else at < mine
        new = combine(
            before, jax.tree.map(lambda part, own: part[at].astype(own.dtype), everything, value)
        )
        return jax.tree.map(lambda a, b: jnp.where(reached, a, b), new, before)

    return lax.fori_loop(0, length, step, start)


def chain_join(earlier, following):
    return (earlier[0] * following[0], following[0][:, None, None] * earlier[1] + following[1])


def causal_filter(stream_rows, previous, kernel_taps):
    rim_rows = previous.shape[0]
    length = stream_rows.shape[0]
    extended = jnp.concatenate([previous, stream_rows], axis=0).astype(jnp.float32)
    result = jnp.zeros(stream_rows.shape, jnp.float32)
    for offset in range(kernel_taps.shape[0]):
        result = (
            result + kernel_taps[offset] * extended[rim_rows - offset : rim_rows - offset + length]
        )
    return result


def filter_back(post_rows, following_rows, kernel_taps):
    length = post_rows.shape[0]
    extended = jnp.concatenate([post_rows, following_rows], axis=0)
    result = jnp.zeros(post_rows.shape, jnp.float32)
    for offset in range(kernel_taps.shape[0]):
        result = result + kernel_taps[offset] * extended[offset : offset + length]
    return result


def tap_sums(post_rows, stream_rows, previous, kernel_width):
    rim_rows = previous.shape[0]
    length = stream_rows.shape[0]
    extended = jnp.concatenate([previous, stream_rows], axis=0).astype(jnp.float32)
    return jnp.stack(
        [
            jnp.sum(post_rows * extended[rim_rows - offset : rim_rows - offset + length], axis=0)
            for offset in range(kernel_width)
        ]
    )


def local(activations, value_weight, query_in, key_in, grad_out, conv_kernel, log_gate):
    tok_rows = query_in.shape[1]
    channels = query_in.shape[2]
    head_count = log_gate.shape[1]
    head_size = channels // head_count
    kernel_width = conv_kernel.shape[1]
    rim_rows = kernel_width - 1
    grad_scale = 1.0 / math.sqrt(lax.axis_size("seq") * lax.axis_size("rep") * tok_rows)
    query_rows = query_in[0]
    key_rows = key_in[0]
    gathered = lax.all_gather(activations, "head", axis=2, tiled=True)[0]
    columns = gathered
    value_f32 = jnp.dot(
        columns,
        lax.all_gather(value_weight, ("seq", "rep"), axis=0, tiled=True),
        preferred_element_type=jnp.float32,
    )
    value_raw = value_f32.astype(jnp.bfloat16)
    before_all = shifted(
        jnp.stack(
            [
                query_rows[tok_rows - rim_rows :],
                key_rows[tok_rows - rim_rows :],
                value_raw[tok_rows - rim_rows :],
            ]
        ),
        "seq",
        1,
    )
    before = (before_all[0], before_all[1], before_all[2])
    raw_rows = (query_rows, key_rows, value_raw)
    convolved = [
        causal_filter(raw_rows[which], before[which], conv_kernel[which]).astype(jnp.bfloat16)
        for which in range(3)
    ]
    query_heads = convolved[0].reshape(tok_rows, head_count, head_size)
    key_heads = convolved[1].reshape(tok_rows, head_count, head_size)
    value_heads = convolved[2].reshape(tok_rows, head_count, head_size)
    cumulative = jnp.cumsum(log_gate[0], axis=1)
    final_cum = cumulative[:, -1]
    block_decay = jnp.exp(final_cum)
    rising = jnp.exp(cumulative).T[:, :, None]
    shrink = jnp.exp(final_cum[:, None] - cumulative).T[:, :, None]
    mixing = jnp.exp(-jnp.abs(cumulative[:, :, None] - cumulative[:, None, :]))
    scores = (
        mixing
        * jnp.einsum("thd,shd->hts", query_heads, key_heads, preferred_element_type=jnp.float32)
    ).astype(jnp.bfloat16)
    fwd_sum = jnp.einsum(
        "thd,the->hde",
        (shrink * key_heads).astype(jnp.bfloat16),
        value_heads,
        preferred_element_type=jnp.float32,
    )
    back_sum = jnp.einsum(
        "thd,the->hde",
        (rising * key_heads).astype(jnp.bfloat16),
        value_heads,
        preferred_element_type=jnp.float32,
    )
    identity = (
        jnp.ones((head_count,), jnp.float32),
        jnp.zeros((head_count, head_size, head_size), jnp.float32),
    )
    left_b = prefix((block_decay, fwd_sum), "seq", chain_join, identity, False)[1].astype(
        jnp.bfloat16
    )
    right_b = prefix((block_decay, back_sum), "seq", chain_join, identity, True)[1].astype(
        jnp.bfloat16
    )
    attn = rising * jnp.einsum(
        "thd,hde->the", query_heads, left_b, preferred_element_type=jnp.float32
    )
    attn = attn + shrink * jnp.einsum(
        "thd,hde->the", query_heads, right_b, preferred_element_type=jnp.float32
    )
    attn = attn + jnp.einsum(
        "hts,she->the", scores, value_heads, preferred_element_type=jnp.float32
    )
    root_mean = jnp.sqrt(jnp.mean(attn * attn, axis=2, keepdims=True) + EPSILON)
    normed = attn / root_mean
    attn_out = normed.astype(jnp.bfloat16).reshape(1, tok_rows, channels)
    upstream = grad_out[0].reshape(tok_rows, head_count, head_size).astype(jnp.float32)
    grad_attn = (
        (upstream - normed * jnp.mean(upstream * normed, axis=2, keepdims=True)) / root_mean
    ).astype(jnp.bfloat16)
    grad_scores = (
        mixing
        * jnp.einsum("the,she->hts", grad_attn, value_heads, preferred_element_type=jnp.float32)
    ).astype(jnp.bfloat16)
    fwd_grad = jnp.einsum(
        "thd,the->hde",
        (shrink * query_heads).astype(jnp.bfloat16),
        grad_attn,
        preferred_element_type=jnp.float32,
    )
    back_grad = jnp.einsum(
        "thd,the->hde",
        (rising * query_heads).astype(jnp.bfloat16),
        grad_attn,
        preferred_element_type=jnp.float32,
    )
    left_gb = carried_in((block_decay, fwd_grad), "seq", chain_join, identity, False)[1].astype(
        jnp.bfloat16
    )
    right_gb = carried_in((block_decay, back_grad), "seq", chain_join, identity, True)[1].astype(
        jnp.bfloat16
    )
    query_post = rising * jnp.einsum(
        "the,hde->thd", grad_attn, left_b, preferred_element_type=jnp.float32
    )
    query_post = query_post + shrink * jnp.einsum(
        "the,hde->thd", grad_attn, right_b, preferred_element_type=jnp.float32
    )
    query_post = query_post + jnp.einsum(
        "hts,shd->thd", grad_scores, key_heads, preferred_element_type=jnp.float32
    )
    key_post = rising * jnp.einsum(
        "the,hde->thd", value_heads, left_gb, preferred_element_type=jnp.float32
    )
    key_post = key_post + shrink * jnp.einsum(
        "the,hde->thd", value_heads, right_gb, preferred_element_type=jnp.float32
    )
    key_post = key_post + jnp.einsum(
        "hts,thd->shd", grad_scores, query_heads, preferred_element_type=jnp.float32
    )
    value_post = rising * jnp.einsum(
        "thd,hde->the", key_heads, left_gb, preferred_element_type=jnp.float32
    )
    value_post = value_post + shrink * jnp.einsum(
        "thd,hde->the", key_heads, right_gb, preferred_element_type=jnp.float32
    )
    value_post = value_post + jnp.einsum(
        "hts,the->she", scores, grad_attn, preferred_element_type=jnp.float32
    )
    post_grads = jnp.stack(
        [
            query_post.reshape(tok_rows, channels),
            key_post.reshape(tok_rows, channels),
            value_post.reshape(tok_rows, channels),
        ]
    )
    following = shifted(post_grads[:, :rim_rows].astype(jnp.bfloat16), "seq", -1).astype(
        jnp.float32
    )
    grad_query = filter_back(post_grads[0], following[0], conv_kernel[0]).astype(jnp.bfloat16)
    grad_key = filter_back(post_grads[1], following[1], conv_kernel[1]).astype(jnp.bfloat16)
    grad_value = filter_back(post_grads[2], following[2], conv_kernel[2]).astype(jnp.bfloat16)
    kernel_terms = (
        jnp.stack(
            [
                tap_sums(post_grads[which], raw_rows[which], before[which], kernel_width)
                for which in range(3)
            ]
        )
        * grad_scale
    )
    grad_conv = lax.psum(kernel_terms, ("seq", "rep"))
    partial_x = lax.dot_general(
        grad_value,
        lax.all_gather(value_weight, ("seq", "rep"), axis=0, tiled=True),
        (((1,), (1,)), ((), ())),
        preferred_element_type=jnp.float32,
    )
    grad_x = lax.psum_scatter(
        partial_x[None].astype(jnp.bfloat16), "head", scatter_dimension=2, tiled=True
    )
    columns = gathered
    grad_w = lax.psum_scatter(
        lax.dot_general(
            columns, grad_value, (((0,), (0,)), ((), ())), preferred_element_type=jnp.float32
        )
        * grad_scale,
        ("seq", "rep"),
        scatter_dimension=0,
        tiled=True,
    )
    return (attn_out, grad_query[None], grad_key[None], grad_x, grad_w, grad_conv)


def solution(mesh):
    placed = (
        P(("parts", "rep"), "seq", "head"),
        P(("seq", "rep"), "head"),
        P(("parts", "rep"), "seq", "head"),
        P(("parts", "rep"), "seq", "head"),
        P(("parts", "rep"), "seq", "head"),
        P(None, None, "head"),
        P(("parts", "rep"), "head", "seq"),
    )
    return jax.shard_map(
        local,
        mesh=mesh,
        in_specs=placed,
        out_specs=(
            P(("parts", "rep"), "seq", "head"),
            P(("parts", "rep"), "seq", "head"),
            P(("parts", "rep"), "seq", "head"),
            P(("parts", "rep"), "seq", "head"),
            P(("parts", "seq", "rep"), "head"),
            P("parts", None, "head"),
        ),
        check_vma=False,
    )
```

profile of v0, /device:TPU:0, one launch (start us, length us, event | category | flops | bytes accessed | tf_op | source)
XLA Modules:
  0.0 710.2 jit_solution(15877381056896727067)
XLA Ops:
  11.9 75.4 %all-gather.12.cloned.1.call-done = bf16[2048,2048]{1,0:T(8,128)(2,1)} async-done(((bf16[128,2048]{1,0:T(8,128)(2,1)}), bf16[2048,2048]{1,0:T(8,128)(2,1)}) %all-gather.12.cloned.1.call-update) | async-done | bytes 8388624 | tf_op jit(solution)/shard_map/all_gather | solution.py:107
  87.2 4.6 convolution_convert_fusion.1
  105.4 16.3 %all-reduce = f32[128]{0:T(128)S(1)} all-reduce(f32[128]{0:T(128)S(1)} %dynamic-update-slice), channel_id=2, replica_groups=mesh['parts'=2,'seq'=8,'rep'=2,'head'=1] {'seq'}, use_global_device_ids=true, to_apply=%add | all-reduce | flops 128 | bytes 1024
  127.9 54.5 %all-gather.14.cloned.1.call-done = f32[128,128,128]{2,1,0:T(8,128)} async-done(((f32[16,128,128]{2,1,0:T(8,128)}), f32[128,128,128]{2,1,0:T(8,128)}) %all-gather.14.cloned.1.call-update) | async-done | bytes 8388624 | tf_op jit(solution)/shard_map/all_gather | solution.py:20
  183.5 2.6 fusion.18
  186.2 78.5 %all-gather.16.cloned.1.call-done = f32[128,128,128]{2,1,0:T(8,128)} async-done(((f32[16,128,128]{2,1,0:T(8,128)}), f32[128,128,128]{2,1,0:T(8,128)}) %all-gather.16.cloned.1.call-update) | async-done | bytes 8388624 | tf_op jit(solution)/shard_map/all_gather | solution.py:20
  265.8 18.6 %while.57 = (s32[]{:T(128)}, f32[16,128,128]{2,1,0:T(8,128)}, s32[]{:T(128)}, f32[8,16]{1,0:T(8,128)S(1)}, f32[8,16,128,128]{3,2,1,0:T(8,128)}, /*index=5*/s32[]{:T(128)}, s32[]{:T(128)}, s32[]{:T(128)}, s32[]{:T(128)}) while((s32[]{:T(128)}, f32[16,128,128]{2,1,0:T(8,128)}, s32[]{:T(128)}, f32[8,16]{1,0:T(8,128)S(1)}, ...), condition=%wide.region_4.5_spmd, body=%wide.region_3.4_spmd.sunk | while | flops 524294 | bytes 3146075 | solution.py:29
  265.8 2.7 bitcast_add_fusion.5
  268.4 2.7 bitcast_add_fusion.5
  271.1 2.7 bitcast_add_fusion.5
  273.8 2.7 bitcast_add_fusion.5
  276.4 2.7 bitcast_add_fusion.5
  279.1 2.7 bitcast_add_fusion.5
  281.7 2.7 bitcast_add_fusion.5
  293.9 14.5 %all-reduce.1 = bf16[128]{0:T(256)(128)(2,1)S(1)} all-reduce(bf16[128]{0:T(256)(128)(2,1)S(1)} %dynamic-update-slice.1), channel_id=7, replica_groups=mesh['parts'=2,'seq'=8,'rep'=2,'head'=1] {'seq'}, use_global_device_ids=true, to_apply=%add.1 | all-reduce | flops 128 | bytes 512
  316.6 19.6 %all-gather.18.cloned.1.call-done = bf16[128,128,128]{2,1,0:T(8,128)(2,1)} async-done(((bf16[16,128,128]{2,1,0:T(8,128)(2,1)}), bf16[128,128,128]{2,1,0:T(8,128)(2,1)}) %all-gather.18.cloned.1.call-update) | async-done | bytes 4194320 | tf_op jit(solution)/shard_map/all_gather | solution.py:35
  336.2 20.2 %while.58 = (s32[]{:T(128)}, f32[16,128,128]{2,1,0:T(8,128)}, s32[]{:T(128)}, bf16[8,16]{1,0:T(8,128)(2,1)S(1)}, bf16[8,16,128,128]{3,2,1,0:T(8,128)(2,1)}, /*index=5*/s32[]{:T(128)}, s32[]{:T(128)}) while((s32[]{:T(128)}, f32[16,128,128]{2,1,0:T(8,128)}, s32[]{:T(128)}, bf16[8,16]{1,0:T(8,128)(2,1)S(1)}, ...), condition=%wide.region_8.9_spmd.clone, body=%wide.region_7.8_spmd.clone.sunk | while | flops 1310740 | bytes 2621713 | solution.py:53
  356.4 2.8 fusion.6
  360.7 22.6 %all-gather.20.cloned.1.call-done = bf16[128,128,128]{2,1,0:T(8,128)(2,1)} async-done(((bf16[16,128,128]{2,1,0:T(8,128)(2,1)}), bf16[128,128,128]{2,1,0:T(8,128)(2,1)}) %all-gather.20.cloned.1.call-update) | async-done | bytes 4194320 | tf_op jit(solution)/shard_map/all_gather | solution.py:35
  383.4 20.9 %while.59 = (s32[]{:T(128)}, f32[16,128,128]{2,1,0:T(8,128)}, s32[]{:T(128)}, bf16[8,16]{1,0:T(8,128)(2,1)S(1)}, bf16[8,16,128,128]{3,2,1,0:T(8,128)(2,1)}, /*index=5*/s32[]{:T(128)}, s32[]{:T(128)}, s32[]{:T(128)}, s32[]{:T(128)}) while((s32[]{:T(128)}, f32[16,128,128]{2,1,0:T(8,128)}, s32[]{:T(128)}, ...), condition=%wide.region_10.11_spmd.clone, body=%wide.region_9.10_spmd.clone.sunk | while | flops 1310744 | bytes 2621775 | solution.py:53
  385.7 2.6 fusion.120
  388.3 2.6 fusion.120
  391.0 2.6 fusion.120
  393.6 2.6 fusion.120
  396.3 2.6 fusion.120
  398.9 2.6 fusion.120
  420.3 3.6 multiply_reduce_fusion.3
  423.9 8.1 %multiply_bitcast_fusion = f32[2048,2048]{0,1:T(8,128)} fusion(bf16[128,2048]{1,0:T(8,128)(2,1)S(1)} %get-tuple-element.476, bf16[1,128,2048]{2,1,0:T(8,128)(2,1)S(1)} %copy-done), kind=kOutput, calls=%fused_computation.10 | convolution fusion | flops 1077936128 | bytes 17825792 | tf_op jit(solution)/shard_map/dot_general | solution.py:262
  438.3 4.3 multiply_reduce_fusion.7
  445.1 8.5 %fusion.2 = bf16[1,128,2048]{2,1,0:T(8,128)(2,1)} fusion(bf16[128,2048]{1,0:T(8,128)(2,1)S(1)} %get-tuple-element.476, bf16[2048,2048]{1,0:T(8,128)(2,1)} %all-gather.12.cloned.1.call-done), kind=kOutput, calls=%fused_computation.13 | convolution fusion | flops 1074003968 | bytes 9437184 | tf_op jit(solution)/shard_map/dot_general | solution.py:251
  453.6 156.4 %reduce-scatter.2.cloned.1.call-done = f32[128,2048]{0,1:T(8,128)} async-done(((f32[2048,2048]{0,1:T(8,128)}), f32[128,2048]{0,1:T(8,128)}) %reduce-scatter.2.cloned.1.call-update) | async-done | bytes 1048592 | tf_op jit(solution)/shard_map/reduce_scatter | solution.py:261
  612.5 89.3 %all-reduce.4.cloned.1.call-done = f32[3,4,2048]{2,1,0:T(4,128)} async-done(((f32[3,4,2048]{2,1,0:T(4,128)}), f32[3,4,2048]{2,1,0:T(4,128)}) %all-reduce.4.cloned.1.call-update) | async-done | bytes 98320 | tf_op jit(solution)/shard_map/psum | solution.py:250
  (168 shorter events, 98.9 us)
Async XLA Ops:
  7.2 80.1 %copy-start = (bf16[1,128,2048]{2,1,0:T(8,128)(2,1)S(1)}, bf16[1,128,2048]{2,1,0:T(8,128)(2,1)}, u32[]{:S(2)}) copy-start(bf16[1,128,2048]{2,1,0:T(8,128)(2,1)} %param.15) | copy-start | bytes 1572868
  7.2 80.1 %all-gather.12.cloned.1.call-start = ((), (), s32[]{:S(2)}) async-start(), calls=%async_computation.1 | async-start | bytes 8912896 | tf_op jit(solution)/shard_map/all_gather | solution.py:107
  7.9 174.5 %all-gather.14.cloned.1.call-start = ((), (), s32[]{:S(2)}) async-start(), calls=%async_computation.4 | async-start | bytes 9437184 | tf_op jit(solution)/shard_map/all_gather | solution.py:20
  11.9 83.1 %copy-start.22 = (bf16[1,128,2048]{2,1,0:T(8,128)(2,1)S(1)}, bf16[1,128,2048]{2,1,0:T(8,128)(2,1)}, u32[]{:S(2)}) copy-start(bf16[1,128,2048]{2,1,0:T(8,128)(2,1)} %param.18) | copy-start | bytes 1572868
  92.0 3.0 collective-permute-start
  97.3 1.9 copy-start.9
  99.2 165.5 %all-gather.16.cloned.1.call-start = ((), (), s32[]{:S(2)}) async-start(), calls=%async_computation.5 | async-start | bytes 9437184 | tf_op jit(solution)/shard_map/all_gather | solution.py:20
  101.5 2.4 copy-start.24
  101.5 20.2 %copy-start.23 = (bf16[1,128,2048]{2,1,0:T(8,128)(2,1)S(1)}, bf16[1,128,2048]{2,1,0:T(8,128)(2,1)}, u32[]{:S(2)}) copy-start(bf16[1,128,2048]{2,1,0:T(8,128)(2,1)} %param.17) | copy-start | bytes 1572868
  101.6 234.7 %all-gather.18.cloned.1.call-start = ((), (), s32[]{:S(2)}) async-start(), calls=%async_computation.6 | async-start | bytes 4718592 | tf_op jit(solution)/shard_map/all_gather | solution.py:35
  121.9 1.1 copy-start.1
  284.4 2.0 copy-start.10
  284.4 2.0 copy-start.20
  286.4 1.2 copy-start.14
  290.9 92.4 %all-gather.20.cloned.1.call-start = ((), (), s32[]{:S(2)}) async-start(), calls=%async_computation.7 | async-start | bytes 4718592 | tf_op jit(solution)/shard_map/all_gather | solution.py:35
  293.3 316.7 %reduce-scatter.2.cloned.1.call-start = ((), (), s32[]{:S(2)}) async-start(), calls=%async_computation.2 | async-start | bytes 17825792 | tf_op jit(solution)/shard_map/reduce_scatter | solution.py:261
  308.5 1.9 copy-start.4
  308.5 1.9 copy-start.7
  310.4 1.7 copy-start.17
  310.4 1.4 copy-start.3
  311.9 1.0 copy-start.13
  356.4 2.8 copy-start.5
  356.4 2.8 copy-start.11
  404.2 2.1 copy-start.8
  404.2 2.2 copy-start.21
  409.9 2.2 copy-start.18
  413.5 2.1 copy-start.19
  416.4 3.9 collective-permute-start.1
  432.0 2.4 copy-start.15
  432.0 269.8 %all-reduce.4.cloned.1.call-start = ((), (), s32[]{:S(2)}) async-start(), calls=%async_computation.3 | async-start | bytes 196608 | tf_op jit(solution)/shard_map/psum | solution.py:250
  438.3 4.3 copy-start.2
  438.3 4.3 copy-start.16
  (2 other events, 1.8 us)
Sparse Core Ops, SparseCore 0:
  10.2 76.9 all-gather.11
  99.3 83.1 all-gather.13
  184.1 80.5 all-gather.15
  291.1 45.1 all-gather.17
  337.7 45.6 all-gather.19
  432.1 177.8 reduce-scatter.1
  614.0 87.7 all-reduce.3
where the time goes:
time: 712 us; the launch traced here: 710 us
  waiting for transfers between devices  498 us (70%)
  other arithmetic  75.9 us (11%)
  matrix products  51.7 us (7%)
  local copies, waits for them, and re-layouts  34.8 us (5%)
  blocking collectives  30.8 us (4%)
  between operations  15.2 us (2%)
    reduce_scatter x1, waiting for transfers between devices, local(): lax.psum_scatter(lax.dot_general(columns, grad_value, (((0,), (0,)), ((),...  156 us
    all_gather x2, waiting for transfers between devices, prefix(): gathered = jax.tree.map(lambda a: lax.all_gather(a, axis), part)  133 us
    psum x1, waiting for transfers between devices, local(): grad_conv = lax.psum(kernel_terms, ('seq', 'rep'))  89.3 us
    all_gather x1, waiting for transfers between devices, local(): lax.all_gather(value_weight, ('seq', 'rep'), axis=0, tiled=True)  75.4 us
    all_gather x2, waiting for transfers between devices, carried_in(): lax.all_gather(part.astype(kind), axis)  42.3 us
    select_n x16, other arithmetic, step(): return jax.tree.map(lambda a, b: jnp.where(reached, a, b), new, before)  40.9 us
    unnamed x2, blocking collectives  30.8 us
    add x7, other arithmetic, chain_join(): following[0][:, None, None] * earlier[1] + following[1]  18.6 us
  transfers between devices with their start and end apart: 9, of which 8 were waited for; matrix products, arithmetic and copies ran while one was open for 11% of the time, Pallas kernels for 0%

commit v1 on v0

--- a/solution.py
+++ b/solution.py
@@ -247,7 +247,7 @@
         )
         * grad_scale
     )
-    grad_conv = lax.psum(kernel_terms, ("seq", "rep"))
+    grad_conv = jnp.sum(lax.all_gather(kernel_terms, ("seq", "rep")), axis=0)
     partial_x = lax.dot_general(
         grad_value,
         lax.all_gather(value_weight, ("seq", "rep"), axis=0, tiled=True),

time: 712 us -> 667 us (0.937)
  waiting for transfers between devices: 498 us -> 453 us
    psum x1 -> x0, waiting for transfers between devices: 89.3 us -> none  [local(): grad_conv = lax.psum(kernel_terms, ('seq', 'rep'))]
    all_gather x0 -> x1, waiting for transfers between devices: none -> 23 us  [local(): grad_conv = jnp.sum(lax.all_gather(kernel_terms, ('seq', 'rep')), axis=0)]
    reduce_scatter x1, waiting for transfers between devices: 156 us -> 178 us  [local(): lax.psum_scatter(lax.dot_general(columns, grad_value, (((0,), (0,)), ((),...]
  transfers between devices with their start and end apart: 9 -> 9, of which waited for: 8 -> 8; matrix products, arithmetic and copies ran while one was open for 11% -> 12% of each run, Pallas kernels for 0% -> 0%
where the time goes in v1:
time: 667 us; the launch traced here: 665 us
  waiting for transfers between devices  453 us (68%)
  other arithmetic  77.1 us (12%)
  matrix products  50.3 us (8%)
  local copies, waits for them, and re-layouts  34.4 us (5%)
  blocking collectives  30.9 us (5%)
  between operations  15.2 us (2%)
    reduce_scatter x1, waiting for transfers between devices, local(): lax.psum_scatter(lax.dot_general(columns, grad_value, (((0,), (0,)), ((),...  178 us
    all_gather x2, waiting for transfers between devices, prefix(): gathered = jax.tree.map(lambda a: lax.all_gather(a, axis), part)  133 us
    all_gather x1, waiting for transfers between devices, local(): lax.all_gather(value_weight, ('seq', 'rep'), axis=0, tiled=True)  75.4 us
    all_gather x2, waiting for transfers between devices, carried_in(): lax.all_gather(part.astype(kind), axis)  42.2 us
    select_n x16, other arithmetic, step(): return jax.tree.map(lambda a, b: jnp.where(reached, a, b), new, before)  40.9 us
    unnamed x2, blocking collectives  30.9 us
    all_gather x1, waiting for transfers between devices, local(): grad_conv = jnp.sum(lax.all_gather(kernel_terms, ('seq', 'rep')), axis=0)  23 us
    add x7, other arithmetic, chain_join(): following[0][:, None, None] * earlier[1] + following[1]  18.6 us
  transfers between devices with their start and end apart: 9, of which 8 were waited for; matrix products, arithmetic and copies ran while one was open for 12% of the time, Pallas kernels for 0%

profile of v1, /device:TPU:0, one launch (start us, length us, event | category | flops | bytes accessed | tf_op | source)
XLA Modules:
  0.0 664.7 jit_solution(7994802415581432285)
XLA Ops:
  11.9 75.4 %all-gather.13.cloned.1.call-done = bf16[2048,2048]{1,0:T(8,128)(2,1)} async-done(((bf16[128,2048]{1,0:T(8,128)(2,1)}), bf16[2048,2048]{1,0:T(8,128)(2,1)}) %all-gather.13.cloned.1.call-update) | async-done | bytes 8388624 | tf_op jit(solution)/shard_map/all_gather | solution.py:107
  87.2 4.6 convolution_convert_fusion.1
  105.4 16.3 %all-reduce = f32[128]{0:T(128)S(1)} all-reduce(f32[128]{0:T(128)S(1)} %dynamic-update-slice), channel_id=2, replica_groups=mesh['parts'=2,'seq'=8,'rep'=2,'head'=1] {'seq'}, use_global_device_ids=true, to_apply=%add | all-reduce | flops 128 | bytes 1024
  127.9 54.5 %all-gather.17.cloned.1.call-done = f32[128,128,128]{2,1,0:T(8,128)} async-done(((f32[16,128,128]{2,1,0:T(8,128)}), f32[128,128,128]{2,1,0:T(8,128)}) %all-gather.17.cloned.1.call-update) | async-done | bytes 8388624 | tf_op jit(solution)/shard_map/all_gather | solution.py:20
  183.5 2.6 fusion.18
  186.2 78.5 %all-gather.19.cloned.1.call-done = f32[128,128,128]{2,1,0:T(8,128)} async-done(((f32[16,128,128]{2,1,0:T(8,128)}), f32[128,128,128]{2,1,0:T(8,128)}) %all-gather.19.cloned.1.call-update) | async-done | bytes 8388624 | tf_op jit(solution)/shard_map/all_gather | solution.py:20
  265.8 18.6 %while.57 = (s32[]{:T(128)}, f32[16,128,128]{2,1,0:T(8,128)}, s32[]{:T(128)}, f32[8,16]{1,0:T(8,128)S(1)}, f32[8,16,128,128]{3,2,1,0:T(8,128)}, /*index=5*/s32[]{:T(128)}, s32[]{:T(128)}, s32[]{:T(128)}, s32[]{:T(128)}) while((s32[]{:T(128)}, f32[16,128,128]{2,1,0:T(8,128)}, s32[]{:T(128)}, f32[8,16]{1,0:T(8,128)S(1)}, ...), condition=%wide.region_4.5_spmd, body=%wide.region_3.4_spmd.sunk | while | flops 524294 | bytes 3146075 | solution.py:29
  265.8 2.7 bitcast_add_fusion.5
  268.4 2.7 bitcast_add_fusion.5
  271.1 2.7 bitcast_add_fusion.5
  273.8 2.7 bitcast_add_fusion.5
  276.4 2.7 bitcast_add_fusion.5
  279.1 2.7 bitcast_add_fusion.5
  281.7 2.7 bitcast_add_fusion.5
  293.9 14.6 %all-reduce.1 = bf16[128]{0:T(256)(128)(2,1)S(1)} all-reduce(bf16[128]{0:T(256)(128)(2,1)S(1)} %dynamic-update-slice.1), channel_id=7, replica_groups=mesh['parts'=2,'seq'=8,'rep'=2,'head'=1] {'seq'}, use_global_device_ids=true, to_apply=%add.1 | all-reduce | flops 128 | bytes 512
  316.8 19.5 %all-gather.21.cloned.1.call-done = bf16[128,128,128]{2,1,0:T(8,128)(2,1)} async-done(((bf16[16,128,128]{2,1,0:T(8,128)(2,1)}), bf16[128,128,128]{2,1,0:T(8,128)(2,1)}) %all-gather.21.cloned.1.call-update) | async-done | bytes 4194320 | tf_op jit(solution)/shard_map/all_gather | solution.py:35
  336.3 20.2 %while.58 = (s32[]{:T(128)}, f32[16,128,128]{2,1,0:T(8,128)}, s32[]{:T(128)}, bf16[8,16]{1,0:T(8,128)(2,1)S(1)}, bf16[8,16,128,128]{3,2,1,0:T(8,128)(2,1)}, /*index=5*/s32[]{:T(128)}, s32[]{:T(128)}) while((s32[]{:T(128)}, f32[16,128,128]{2,1,0:T(8,128)}, s32[]{:T(128)}, bf16[8,16]{1,0:T(8,128)(2,1)S(1)}, ...), condition=%wide.region_8.9_spmd.clone, body=%wide.region_7.8_spmd.clone.sunk | while | flops 1310740 | bytes 2621713 | solution.py:53
  356.5 2.8 fusion.6
  360.8 22.6 %all-gather.23.cloned.1.call-done = bf16[128,128,128]{2,1,0:T(8,128)(2,1)} async-done(((bf16[16,128,128]{2,1,0:T(8,128)(2,1)}), bf16[128,128,128]{2,1,0:T(8,128)(2,1)}) %all-gather.23.cloned.1.call-update) | async-done | bytes 4194320 | tf_op jit(solution)/shard_map/all_gather | solution.py:35
  383.4 20.9 %while.59 = (s32[]{:T(128)}, f32[16,128,128]{2,1,0:T(8,128)}, s32[]{:T(128)}, bf16[8,16]{1,0:T(8,128)(2,1)S(1)}, bf16[8,16,128,128]{3,2,1,0:T(8,128)(2,1)}, /*index=5*/s32[]{:T(128)}, s32[]{:T(128)}, s32[]{:T(128)}, s32[]{:T(128)}) while((s32[]{:T(128)}, f32[16,128,128]{2,1,0:T(8,128)}, s32[]{:T(128)}, ...), condition=%wide.region_10.11_spmd.clone, body=%wide.region_9.10_spmd.clone.sunk | while | flops 1310744 | bytes 2621775 | solution.py:53
  385.8 2.6 fusion.120
  388.4 2.6 fusion.120
  391.1 2.6 fusion.120
  393.7 2.6 fusion.120
  396.4 2.6 fusion.120
  399.0 2.6 fusion.120
  401.7 2.6 fusion.120
  425.6 5.6 multiply_reduce_fusion.11
  435.0 8.1 %multiply_bitcast_fusion = f32[2048,2048]{0,1:T(8,128)} fusion(bf16[128,2048]{1,0:T(8,128)(2,1)S(1)} %get-tuple-element.476, bf16[1,128,2048]{2,1,0:T(8,128)(2,1)S(1)} %copy-done), kind=kOutput, calls=%fused_computation.10 | convolution fusion | flops 1077936128 | bytes 17825792 | tf_op jit(solution)/shard_map/dot_general | solution.py:262
  445.2 7.1 %fusion.2 = bf16[1,128,2048]{2,1,0:T(8,128)(2,1)} fusion(bf16[128,2048]{1,0:T(8,128)(2,1)S(1)} %get-tuple-element.476, bf16[2048,2048]{1,0:T(8,128)(2,1)} %all-gather.13.cloned.1.call-done), kind=kOutput, calls=%fused_computation.13 | convolution fusion | flops 1074003968 | bytes 9437184 | tf_op jit(solution)/shard_map/dot_general | solution.py:251
  452.2 23.0 %all-gather.15.cloned.1.call-done = f32[16,3,4,2048]{3,2,1,0:T(4,128)} async-done(((f32[1,3,4,2048]{3,2,1,0:T(4,128)}), f32[16,3,4,2048]{3,2,1,0:T(4,128)}) %all-gather.15.cloned.1.call-update) | async-done | bytes 1572880 | tf_op jit(solution)/shard_map/all_gather | solution.py:250
  477.6 177.6 %reduce-scatter.2.cloned.1.call-done = f32[128,2048]{0,1:T(8,128)} async-done(((f32[2048,2048]{0,1:T(8,128)}), f32[128,2048]{0,1:T(8,128)}) %reduce-scatter.2.cloned.1.call-update) | async-done | bytes 1048592 | tf_op jit(solution)/shard_map/reduce_scatter | solution.py:261
  (168 shorter events, 99.4 us)
Async XLA Ops:
  7.2 80.1 %copy-start = (bf16[1,128,2048]{2,1,0:T(8,128)(2,1)S(1)}, bf16[1,128,2048]{2,1,0:T(8,128)(2,1)}, u32[]{:S(2)}) copy-start(bf16[1,128,2048]{2,1,0:T(8,128)(2,1)} %param.15) | copy-start | bytes 1572868
  7.2 80.1 %all-gather.13.cloned.1.call-start = ((), (), s32[]{:S(2)}) async-start(), calls=%async_computation.1 | async-start | bytes 8912896 | tf_op jit(solution)/shard_map/all_gather | solution.py:107
  7.9 174.5 %all-gather.17.cloned.1.call-start = ((), (), s32[]{:S(2)}) async-start(), calls=%async_computation.4 | async-start | bytes 9437184 | tf_op jit(solution)/shard_map/all_gather | solution.py:20
  11.9 83.2 %copy-start.22 = (bf16[1,128,2048]{2,1,0:T(8,128)(2,1)S(1)}, bf16[1,128,2048]{2,1,0:T(8,128)(2,1)}, u32[]{:S(2)}) copy-start(bf16[1,128,2048]{2,1,0:T(8,128)(2,1)} %param.18) | copy-start | bytes 1572868
  92.0 3.0 collective-permute-start
  96.8 1.0 copy-start.11
  97.3 1.9 copy-start.8
  99.2 165.5 %all-gather.19.cloned.1.call-start = ((), (), s32[]{:S(2)}) async-start(), calls=%async_computation.5 | async-start | bytes 9437184 | tf_op jit(solution)/shard_map/all_gather | solution.py:20
  101.5 2.4 copy-start.24
  101.5 20.2 %copy-start.23 = (bf16[1,128,2048]{2,1,0:T(8,128)(2,1)S(1)}, bf16[1,128,2048]{2,1,0:T(8,128)(2,1)}, u32[]{:S(2)}) copy-start(bf16[1,128,2048]{2,1,0:T(8,128)(2,1)} %param.17) | copy-start | bytes 1572868
  101.6 234.8 %all-gather.21.cloned.1.call-start = ((), (), s32[]{:S(2)}) async-start(), calls=%async_computation.6 | async-start | bytes 4718592 | tf_op jit(solution)/shard_map/all_gather | solution.py:35
  121.9 1.1 copy-start.1
  284.4 2.0 copy-start.9
  284.4 2.0 copy-start.19
  286.4 1.2 copy-start.13
  291.0 92.4 %all-gather.23.cloned.1.call-start = ((), (), s32[]{:S(2)}) async-start(), calls=%async_computation.7 | async-start | bytes 4718592 | tf_op jit(solution)/shard_map/all_gather | solution.py:35
  293.4 181.9 %all-gather.15.cloned.1.call-start = ((), (), s32[]{:S(2)}) async-start(), calls=%async_computation.3 | async-start | bytes 1671168 | tf_op jit(solution)/shard_map/all_gather | solution.py:250
  308.7 1.9 copy-start.2
  308.7 1.9 copy-start.6
  310.6 1.7 copy-start.16
  310.6 1.4 copy-start.3
  356.5 2.8 copy-start.4
  356.5 2.8 copy-start.10
  404.3 2.1 copy-start.7
  404.3 2.2 copy-start.20
  409.9 2.2 copy-start.17
  413.6 2.1 copy-start.18
  416.5 9.0 %collective-permute-start.1 = (bf16[3,3,2048]{2,1,0:T(4,128)(2,1)S(1)}, bf16[3,3,2048]{2,1,0:T(4,128)(2,1)S(1)}, u32[]{:S(2)}, u32[]{:S(2)}) collective-permute-start(bf16[3,3,2048]{2,1,0:T(4,128)(2,1)S(1)} %pad_maximum_fusion.3), channel_id=1, source_target_pairs={{2,0},{4,2},{6,4},{8,6},{10,8},{12,10},{14,12},{3,1},{5,3},{7,5},{... | collective-permute-start | bytes 110600 | tf_op jit(solution)/shard_map/ppermute | solution.py:13
  425.5 5.6 copy-start.15
  431.2 1.7 copy-start.14
  434.8 220.5 %reduce-scatter.2.cloned.1.call-start = ((), (), s32[]{:S(2)}) async-start(), calls=%async_computation.2 | async-start | bytes 17825792 | tf_op jit(solution)/shard_map/reduce_scatter | solution.py:261
  443.1 1.0 copy-start.21
  (2 other events, 1.9 us)
Sparse Core Ops, SparseCore 0:
  10.2 76.9 all-gather.12
  99.3 83.1 all-gather.16
  184.1 80.5 all-gather.18
  291.1 45.1 all-gather.20
  337.8 45.6 all-gather.22
  434.9 40.3 all-gather.14
  479.4 175.8 reduce-scatter.1
